TPU v7x, 32 devices: a whole 2x2x4 slice. The times are simulated.
32 devices in a mesh: seq: 16 (over z, y, core), head: 2 (over x).
Axes of the slice: x: 2, y: 2, z: 4, core: 2. Of those that a mesh axis runs over, the one named last changes fastest.
Arguments:
- queries: bfloat16 [8192, 4096], P('seq', 'head'), may hold values from -20 to 20
- key_rows: bfloat16 [8192, 2048], P('seq', 'head'), may hold values from -20 to 20
- values: bfloat16 [8192, 2048], P('seq', 'head'), may hold values from -24 to 24
- out_weight: bfloat16 [4096, 5376], P('head'), may hold values from -0.09375 to 0.09375
Outputs:
- projected: bfloat16 [8192, 5376], P(('seq', 'head'))
All inputs are finite; a program needn't handle non-finite values.
Results may differ from a plain program's by a relative error of at most 0.019.
Values may be sent and summed in bfloat16 or wider, within the bound.
A program may use at most 192 MiB of HBM per device.

v0:
```python
import jax
import jax.numpy as jnp
from jax import lax
from jax.sharding import PartitionSpec as P

HD = 128
attn_scale = 168.0 ** (-0.5)
neg_fill = -1e30
key_block = 512


def from_behind(value, axis, steps):
    count = lax.axis_size(axis)
    leading, last = (max(0, -steps), min(count, count - steps))
    return lax.ppermute(value, axis, [(source, source + steps) for source in range(leading, last)])


def for_sending(x):

    def short(part):
        return part.astype(jnp.bfloat16) if part.dtype == jnp.float32 else part

    return jax.tree.map(short, x)


def attend(states, query_part, query_begin, key_part, value_part, key_begin, key_low, key_high):
    query_len = query_part.shape[0]
    key_len = key_part.shape[0]
    needed = (
        (key_begin <= query_begin + query_len - 1)
        & (key_begin + key_len > key_low)
        & (key_begin < key_high)
    )

    def compute(states):
        row_max, row_sum, summed = states
        query_pos = query_begin + jnp.arange(query_len, dtype=jnp.int32)
        key_pos = key_begin + jnp.arange(key_len, dtype=jnp.int32)
        allowed = (
            (key_pos[None, :] <= query_pos[:, None])
            & (key_pos[None, :] >= key_low)
            & (key_pos[None, :] < key_high)
        )
        scores = (
            jnp.einsum("qhgd,khd->hgqk", query_part, key_part, preferred_element_type=jnp.float32)
            * attn_scale
        )
        scores = jnp.where(allowed[None, None], scores, neg_fill)
        new_max = jnp.maximum(row_max, jnp.max(scores, axis=-1))
        weights = jnp.where(allowed[None, None], jnp.exp(scores - new_max[..., None]), 0.0)
        factor = jnp.exp(row_max - new_max)
        new_sum = row_sum * factor + jnp.sum(weights, axis=-1)
        rounded = weights.astype(jnp.bfloat16)
        new_summed = summed * factor[..., None] + jnp.einsum(
            "hgqk,khd->hgqd", rounded, value_part, preferred_element_type=jnp.float32
        )
        return (new_max, new_sum, new_summed)

    return lax.cond(needed, compute, lambda kept: kept, states)


def fresh_state(value_heads, per_group, local_rows):
    return (
        jnp.full((value_heads, per_group, local_rows), neg_fill, jnp.float32),
        jnp.zeros((value_heads, per_group, local_rows), jnp.float32),
        jnp.zeros((value_heads, per_group, local_rows, HD), jnp.float32),
    )


def per_device(queries, key_rows, values, out_weight):
    spans = lax.axis_size("seq")
    myself = lax.axis_index("seq")
    local_rows = queries.shape[0]
    value_heads = key_rows.shape[1] // HD
    query_heads = queries.shape[1] // HD
    per_group = query_heads // value_heads
    own_grid = queries.reshape(local_rows, value_heads, per_group, HD)
    own_begin = myself * local_rows
    query_sets = []
    half_axis = spans // 2
    lent_limit = spans // 4 * local_rows
    is_late = myself >= half_axis
    own_low = jnp.where(is_late, lent_limit, 0).astype(jnp.int32)
    query_sets.append((own_grid, own_begin, own_low, jnp.int32(2**30)))
    lent = from_behind(queries, "seq", -half_axis)
    lent_grid = lent.reshape(local_rows, value_heads, per_group, HD)
    lent_high = jnp.where(is_late, 0, lent_limit).astype(jnp.int32)
    query_sets.append((lent_grid, (myself + half_axis) * local_rows, jnp.int32(0), lent_high))
    initial = tuple((fresh_state(value_heads, per_group, local_rows) for entry in query_sets))
    key_piece = lax.all_gather(key_rows, "seq", axis=0, tiled=True)
    value_piece = lax.all_gather(values, "seq", axis=0, tiled=True)
    piece_rows = key_piece.shape[0]
    block_total = piece_rows // key_block

    def advance(block_id, inner):
        key_slab = lax.dynamic_slice_in_dim(key_piece, block_id * key_block, key_block, 0).reshape(
            key_block, value_heads, HD
        )
        value_slab = lax.dynamic_slice_in_dim(
            value_piece, block_id * key_block, key_block, 0
        ).reshape(key_block, value_heads, HD)
        key_begin = block_id * key_block
        return tuple(
            (
                attend(state_one, grid, begin, key_slab, value_slab, key_begin, lower, upper)
                for state_one, (grid, begin, lower, upper) in zip(inner, query_sets)
            )
        )

    results = lax.fori_loop(0, block_total, advance, initial)
    row_max, row_sum, summed = results[0]
    back_max, back_sum, back_summed = from_behind(for_sending(results[1]), "seq", spans // 2)
    back_max = jnp.where(myself >= spans // 2, back_max, neg_fill)
    joint_max = jnp.maximum(row_max, back_max)
    own_factor = jnp.exp(row_max - joint_max)
    back_factor = jnp.exp(back_max - joint_max)
    row_sum = row_sum * own_factor + back_sum * back_factor
    summed = summed * own_factor[..., None] + back_summed * back_factor[..., None]
    attended = (
        (summed / row_sum[..., None])
        .transpose(2, 0, 1, 3)
        .reshape(local_rows, query_heads * HD)
        .astype(jnp.bfloat16)
    )
    return lax.psum_scatter(
        jnp.dot(attended, out_weight, preferred_element_type=jnp.float32).astype(jnp.bfloat16),
        "head",
        scatter_dimension=0,
        tiled=True,
    )


def solution(mesh):
    placed = (P("seq", "head"), P("seq", "head"), P("seq", "head"), P("head", None))
    return jax.shard_map(
        per_device, mesh=mesh, in_specs=placed, out_specs=P(("seq", "head"), None), check_vma=False
    )
```

profile of v0, /device:TPU:0, one launch (start us, length us, event | category | flops | bytes accessed | tf_op | source)
XLA Modules:
  0.0 802.0 jit_solution(6045147930715456967)
XLA Ops:
  11.3 3.9 copy.15
  16.5 3.1 copy.17
  19.6 179.8 %collective-permute-done = bf16[512,2048]{0,1:T(8,128)(2,1)} collective-permute-done((bf16[512,2048]{0,1:T(8,128)(2,1)}, bf16[512,2048]{0,1:T(8,128)(2,1)}, u32[]{:S(2)}, u32[]{:S(2)}) %collective-permute-start) | collective-permute-done | bytes 2097184 | tf_op jit(solution)/shard_map/ppermute | solution.py:15
  199.4 3.9 copy.18
  203.3 14.5 %all-gather.3.cloned.1.call-done = bf16[8192,1024]{0,1:T(8,128)(2,1)} async-done(((bf16[512,1024]{0,1:T(8,128)(2,1)}), bf16[8192,1024]{0,1:T(8,128)(2,1)}) %all-gather.3.cloned.1.call-update) | async-done | bytes 16777232 | tf_op jit(solution)/shard_map/all_gather | solution.py:90
  217.8 133.6 %all-gather.5.cloned.1.call-done = bf16[8192,1024]{0,1:T(8,128)(2,1)} async-done(((bf16[512,1024]{0,1:T(8,128)(2,1)}), bf16[8192,1024]{0,1:T(8,128)(2,1)}) %all-gather.5.cloned.1.call-update) | async-done | bytes 16777232 | tf_op jit(solution)/shard_map/all_gather | solution.py:91
  356.4 161.2 %while.26 = (s32[]{:T(128)}, f32[8,2,512]{2,1,0:T(2,128)S(1)}, f32[8,2,512]{2,1,0:T(2,128)S(1)}, f32[8,2,512,128]{3,2,1,0:T(8,128)}, f32[8,2,512]{2,1,0:T(2,128)...) while((s32[]{:T(128)}, f32[8,2,512]{2,1,0:T(2,128)S(1)}, ...), condition=%wide.region_9.10_spmd, body=%wide.region_0.9_spmd.sunk | while | flops 4409824256 | bytes 342905664 | solution.py:110
  356.4 2.7 constant_dynamic-slice_fusion.3
  359.1 22.8 %conditional.4 = ((f32[8,2,512]{2,1,0:T(2,128)S(1)}, f32[8,2,512]{2,1,0:T(2,128)S(1)}, f32[8,2,512,128]{3,2,1,0:T(8,128)})) conditional(s32[]{:T(128)} %convert_element_type.91, (f32[8,2,512]{2,1,0:T(2,128)S(1)}, f32[8,2,512]{2,1,0:T(2,128)S(1)}, f32[8,2,512,128]{3,2,1,0:T(8,128)}) %tuple.74, (s32[]{:T(128)}, s32[]{:T(128)}, s32[]{:T(128)}, ...), branch_computations={%region_1.1_spmd, %region_2.4_spmd} | conditional | flops 2204912128 | bytes 169355424 | solution.py:59
  359.4 3.8 fusion
  363.2 4.0 fusion.2
  367.2 3.3 copy-done
  370.6 9.2 %multiply_add_fusion = f32[8,2,512,128]{3,2,1,0:T(8,128)S(1)} fusion(f32[8,2,512,128]{3,2,1,0:T(8,128)S(1)} %copy-done.6, f32[8,2,512]{2,1,0:T(2,128)S(1)} %bitcast.92, f32[8,512,512,2]{2,1,3,0:T(8,128)} %copy-done, f32[8,2,512]{2,1,0:T(2,128)S(1)} %max.6, pred[512,512]{0,1:T(8,128)(4,1)S(1)} %and_and_fusion, bf16[512,8,128]{0,2,1:T(8,128)(2,1)S(1)} %copy-done.2), kind=kOutput, calls=%fused_computation.7 | convolution fusion | flops 1096810496 | bytes 26542080 | tf_op jit(solution)/shard_map/while/body/eval_jaxpr/cond/branch_1_fun/hgqk,khd->hgqd/dot_general | solution.py:54
  381.9 24.0 %conditional.5 = ((f32[8,2,512]{2,1,0:T(2,128)S(1)}, f32[8,2,512]{2,1,0:T(2,128)S(1)}, f32[8,2,512,128]{3,2,1,0:T(8,128)})) conditional(s32[]{:T(128)} %convert_element_type.92, (f32[8,2,512]{2,1,0:T(2,128)S(1)}, f32[8,2,512]{2,1,0:T(2,128)S(1)}, f32[8,2,512,128]{3,2,1,0:T(8,128)}) %tuple.76, (s32[]{:T(128)}, s32[]{:T(128)}, s32[]{:T(128)}, ...), branch_computations={%region_5.5_spmd, %region_6.8_spmd} | conditional | flops 2204912128 | bytes 169355424 | solution.py:59
  382.2 5.0 fusion.16
  387.2 4.0 fusion.18
  391.3 3.3 copy-done.1
  394.7 9.2 %multiply_add_fusion.2 = f32[8,2,512,128]{3,2,1,0:T(8,128)S(1)} fusion(f32[8,2,512,128]{3,2,1,0:T(8,128)S(1)} %copy-done.4, f32[8,2,512]{2,1,0:T(2,128)S(1)} %bitcast.93, f32[8,512,512,2]{2,1,3,0:T(8,128)} %copy-done.1, f32[8,2,512]{2,1,0:T(2,128)S(1)} %max.7, pred[512,512]{0,1:T(8,128)(4,1)S(1)} %and_and_fusion.1, bf16[512,8,128]{0,2,1:T(8,128)(2,1)S(1)} %copy-done.3), kind=kOutput, calls=%fused_computation.28 | convolution fusion | flops 1096810496 | bytes 26542080 | tf_op jit(solution)/shard_map/while/body/eval_jaxpr/cond/branch_1_fun/hgqk,khd->hgqd/dot_general | solution.py:54
  405.8 2.7 constant_dynamic-slice_fusion.3
  408.5 24.0 %conditional.5 = ((f32[8,2,512]{2,1,0:T(2,128)S(1)}, f32[8,2,512]{2,1,0:T(2,128)S(1)}, f32[8,2,512,128]{3,2,1,0:T(8,128)})) conditional(s32[]{:T(128)} %convert_element_type.92, (f32[8,2,512]{2,1,0:T(2,128)S(1)}, f32[8,2,512]{2,1,0:T(2,128)S(1)}, f32[8,2,512,128]{3,2,1,0:T(8,128)}) %tuple.76, (s32[]{:T(128)}, s32[]{:T(128)}, s32[]{:T(128)}, ...), branch_computations={%region_5.5_spmd, %region_6.8_spmd} | conditional | flops 2204912128 | bytes 169355424 | solution.py:59
  408.8 5.0 fusion.16
  413.9 4.0 fusion.18
  417.9 3.3 copy-done.1
  421.3 9.2 %multiply_add_fusion.2 = f32[8,2,512,128]{3,2,1,0:T(8,128)S(1)} fusion(f32[8,2,512,128]{3,2,1,0:T(8,128)S(1)} %copy-done.4, f32[8,2,512]{2,1,0:T(2,128)S(1)} %bitcast.93, f32[8,512,512,2]{2,1,3,0:T(8,128)} %copy-done.1, f32[8,2,512]{2,1,0:T(2,128)S(1)} %max.7, pred[512,512]{0,1:T(8,128)(4,1)S(1)} %and_and_fusion.1, bf16[512,8,128]{0,2,1:T(8,128)(2,1)S(1)} %copy-done.3), kind=kOutput, calls=%fused_computation.28 | convolution fusion | flops 1096810496 | bytes 26542080 | tf_op jit(solution)/shard_map/while/body/eval_jaxpr/cond/branch_1_fun/hgqk,khd->hgqd/dot_general | solution.py:54
  432.5 2.7 constant_dynamic-slice_fusion.3
  435.1 24.0 %conditional.5 = ((f32[8,2,512]{2,1,0:T(2,128)S(1)}, f32[8,2,512]{2,1,0:T(2,128)S(1)}, f32[8,2,512,128]{3,2,1,0:T(8,128)})) conditional(s32[]{:T(128)} %convert_element_type.92, (f32[8,2,512]{2,1,0:T(2,128)S(1)}, f32[8,2,512]{2,1,0:T(2,128)S(1)}, f32[8,2,512,128]{3,2,1,0:T(8,128)}) %tuple.76, (s32[]{:T(128)}, s32[]{:T(128)}, s32[]{:T(128)}, ...), branch_computations={%region_5.5_spmd, %region_6.8_spmd} | conditional | flops 2204912128 | bytes 169355424 | solution.py:59
  435.4 5.0 fusion.16
  440.5 4.0 fusion.18
  444.5 3.3 copy-done.1
  447.9 9.2 %multiply_add_fusion.2 = f32[8,2,512,128]{3,2,1,0:T(8,128)S(1)} fusion(f32[8,2,512,128]{3,2,1,0:T(8,128)S(1)} %copy-done.4, f32[8,2,512]{2,1,0:T(2,128)S(1)} %bitcast.93, f32[8,512,512,2]{2,1,3,0:T(8,128)} %copy-done.1, f32[8,2,512]{2,1,0:T(2,128)S(1)} %max.7, pred[512,512]{0,1:T(8,128)(4,1)S(1)} %and_and_fusion.1, bf16[512,8,128]{0,2,1:T(8,128)(2,1)S(1)} %copy-done.3), kind=kOutput, calls=%fused_computation.28 | convolution fusion | flops 1096810496 | bytes 26542080 | tf_op jit(solution)/shard_map/while/body/eval_jaxpr/cond/branch_1_fun/hgqk,khd->hgqd/dot_general | solution.py:54
  459.1 2.7 constant_dynamic-slice_fusion.3
  461.8 24.0 %conditional.5 = ((f32[8,2,512]{2,1,0:T(2,128)S(1)}, f32[8,2,512]{2,1,0:T(2,128)S(1)}, f32[8,2,512,128]{3,2,1,0:T(8,128)})) conditional(s32[]{:T(128)} %convert_element_type.92, (f32[8,2,512]{2,1,0:T(2,128)S(1)}, f32[8,2,512]{2,1,0:T(2,128)S(1)}, f32[8,2,512,128]{3,2,1,0:T(8,128)}) %tuple.76, (s32[]{:T(128)}, s32[]{:T(128)}, s32[]{:T(128)}, ...), branch_computations={%region_5.5_spmd, %region_6.8_spmd} | conditional | flops 2204912128 | bytes 169355424 | solution.py:59
  462.1 5.0 fusion.16
  467.1 4.0 fusion.18
  471.2 3.3 copy-done.1
  474.6 9.2 %multiply_add_fusion.2 = f32[8,2,512,128]{3,2,1,0:T(8,128)S(1)} fusion(f32[8,2,512,128]{3,2,1,0:T(8,128)S(1)} %copy-done.4, f32[8,2,512]{2,1,0:T(2,128)S(1)} %bitcast.93, f32[8,512,512,2]{2,1,3,0:T(8,128)} %copy-done.1, f32[8,2,512]{2,1,0:T(2,128)S(1)} %max.7, pred[512,512]{0,1:T(8,128)(4,1)S(1)} %and_and_fusion.1, bf16[512,8,128]{0,2,1:T(8,128)(2,1)S(1)} %copy-done.3), kind=kOutput, calls=%fused_computation.28 | convolution fusion | flops 1096810496 | bytes 26542080 | tf_op jit(solution)/shard_map/while/body/eval_jaxpr/cond/branch_1_fun/hgqk,khd->hgqd/dot_general | solution.py:54
  485.7 2.7 constant_dynamic-slice_fusion.3
  488.4 2.7 constant_dynamic-slice_fusion.3
  491.0 2.7 constant_dynamic-slice_fusion.3
  493.7 2.7 constant_dynamic-slice_fusion.3
  499.0 2.7 constant_dynamic-slice_fusion.3
  501.7 2.7 constant_dynamic-slice_fusion.3
  517.6 3.3 copy.20
  526.4 5.3 copy.19
  531.8 14.5 %collective-permute-done.3 = bf16[8,2,512]{2,1,0:T(2,128)(2,1)S(1)} collective-permute-done((bf16[8,2,512]{2,1,0:T(2,128)(2,1)S(1)}, bf16[8,2,512]{2,1,0:T(2,128)(2,1)S(1)}, u32[]{:S(2)}, u32[]{:S(2)}) %collective-permute-start.3) | collective-permute-done | bytes 16416 | tf_op jit(solution)/shard_map/ppermute | solution.py:15
  546.7 3.7 divide_convert_fusion
  550.5 18.6 %convolution_convert_fusion = bf16[512,5376]{1,0:T(8,128)(2,1)} fusion(bf16[512,2048]{0,1:T(8,128)(2,1)S(1)} %bitcast.87, bf16[2048,5376]{1,0:T(8,128)(2,1)} %param.13), kind=kOutput, calls=%fused_computation.44 | convolution fusion | flops 11277041664 | bytes 29622272 | tf_op jit(solution)/shard_map/dot_general | solution.py:126
  569.0 226.5 %reduce-scatter.2.cloned.1.call-done = bf16[256,5376]{1,0:T(8,128)(2,1)} async-done(((bf16[512,5376]{1,0:T(8,128)(2,1)}), bf16[256,5376]{1,0:T(8,128)(2,1)}) %reduce-scatter.2.cloned.1.call-update) | async-done | bytes 2752528 | tf_op jit(solution)/shard_map/reduce_scatter | solution.py:125
  (121 shorter events, 44.5 us)
Async XLA Ops:
  6.5 211.2 %all-gather.3.cloned.1.call-start = ((), (), s32[]{:S(2)}) async-start(), calls=%async_computation.1 | async-start | bytes 17825792 | tf_op jit(solution)/shard_map/all_gather | solution.py:90
  8.8 342.5 %all-gather.5.cloned.1.call-start = ((), (), s32[]{:S(2)}) async-start(), calls=%async_computation.2 | async-start | bytes 17825792 | tf_op jit(solution)/shard_map/all_gather | solution.py:91
  11.2 784.3 %reduce-scatter.2.cloned.1.call-start = ((), (), s32[]{:S(2)}) async-start(), calls=%async_computation.3 | async-start | bytes 8257536 | tf_op jit(solution)/shard_map/reduce_scatter | solution.py:125
  15.2 184.2 %collective-permute-start = (bf16[512,2048]{0,1:T(8,128)(2,1)}, bf16[512,2048]{0,1:T(8,128)(2,1)}, u32[]{:S(2)}, u32[]{:S(2)}) collective-permute-start(bf16[512,2048]{0,1:T(8,128)(2,1)} %copy.15), channel_id=1, source_target_pairs={{16,0},{18,2},{20,4},{22,6},{24,8},{26,10},{28,12},{30,14},{17,1},... | collective-permute-start | bytes 6291464 | tf_op jit(solution)/shard_map/ppermute | solution.py:15
  363.1 7.4 copy-start
  363.2 7.4 copy-start.2
  363.2 7.4 copy-start.6
  379.8 2.1 copy-start.7
  387.2 7.4 copy-start.1
  387.2 7.4 copy-start.3
  387.2 7.4 copy-start.4
  403.8 2.0 copy-start.5
  413.8 7.4 copy-start.1
  413.8 7.4 copy-start.3
  413.8 7.4 copy-start.4
  430.5 2.0 copy-start.5
  440.4 7.4 copy-start.1
  440.5 7.4 copy-start.3
  440.5 7.4 copy-start.4
  457.1 2.0 copy-start.5
  467.1 7.4 copy-start.1
  467.1 7.4 copy-start.3
  467.1 7.4 copy-start.4
  483.7 2.0 copy-start.5
  521.0 25.7 %collective-permute-start.2 = (bf16[8,2,512,128]{2,3,1,0:T(8,128)(2,1)S(1)}, bf16[8,2,512,128]{2,3,1,0:T(8,128)(2,1)}, u32[]{:S(2)}, u32[]{:S(2)}) collective-permute-start(bf16[8,2,512,128]{2,3,1,0:T(8,128)(2,1)S(1)} %copy.20), channel_id=1, source_target_pairs={{0,16},{2,18},{4,20},{6,22},{8,24},{10,26},{12,28},{14,30},{1,17},... | collective-permute-start | bytes 6291464 | tf_op jit(solution)/shard_map/ppermute | solution.py:15
  523.6 22.6 %collective-permute-start.3 = (bf16[8,2,512]{2,1,0:T(2,128)(2,1)S(1)}, bf16[8,2,512]{2,1,0:T(2,128)(2,1)S(1)}, u32[]{:S(2)}, u32[]{:S(2)}) collective-permute-start(bf16[8,2,512]{2,1,0:T(2,128)(2,1)S(1)} %convert_element_type.63), channel_id=1, source_target_pairs={{0,16},{2,18},{4,20},{6,22},{8,24},{10,26},{12,28},{14,30},{1,17},... | collective-permute-start | bytes 49160 | tf_op jit(solution)/shard_map/ppermute | solution.py:15
  525.1 21.5 %collective-permute-start.1 = (bf16[8,2,512]{2,1,0:T(2,128)(2,1)S(1)}, bf16[8,2,512]{2,1,0:T(2,128)(2,1)S(1)}, u32[]{:S(2)}, u32[]{:S(2)}) collective-permute-start(bf16[8,2,512]{2,1,0:T(2,128)(2,1)S(1)} %convert_element_type.59), channel_id=1, source_target_pairs={{0,16},{2,18},{4,20},{6,22},{8,24},{10,26},{12,28},{14,30},{1,17},... | collective-permute-start | bytes 49160 | tf_op jit(solution)/shard_map/ppermute | solution.py:15
Sparse Core Ops, SparseCore 0:
  9.5 208.2 all-gather.2
  219.9 131.4 all-gather.4
  569.1 226.2 reduce-scatter.1
where the time goes:
time: 804 us; the launch traced here: 802 us
  waiting for transfers between devices  569 us (71%)
  local copies, waits for them, and re-layouts  98.4 us (12%)
  matrix products  88.1 us (11%)
  other arithmetic  25.7 us (3%)
  between operations  13.2 us (2%)
    reduce_scatter x1, waiting for transfers between devices, per_device(): lax.psum_scatter(jnp.dot(attended, out_weight, preferred_element_type=jnp...  226 us
    ppermute x4, waiting for transfers between devices, from_behind(): lax.ppermute(value, axis, [(source, source + steps) for source in range(l...  195 us
    all_gather x1, waiting for transfers between devices, per_device(): value_piece = lax.all_gather(values, 'seq', axis=0, tiled=True)  134 us
    dot_general x5, matrix products, compute(): jnp.einsum('hgqk,khd->hgqd', rounded, value_part, preferred_element_type=...  45.8 us
    dynamic_slice x16, local copies, waits for them, and re-layouts, advance(): lax.dynamic_slice_in_dim(value_piece, block_id * key_block, key_block, 0)  42.5 us
    cond x45, local copies, waits for them, and re-layouts  26.8 us
    dot_general x5, matrix products, compute(): jnp.einsum('qhgd,khd->hgqk', query_part, key_part, preferred_element_type...  23.7 us
    reduce_sum x5, other arithmetic, compute(): new_sum = row_sum * factor + jnp.sum(weights, axis=-1)  20.2 us
  transfers between devices with their start and end apart: 7, of which 6 were waited for; matrix products, arithmetic and copies ran while one was open for 2% of the time, Pallas kernels for 0%

commit v1 on v0

--- a/solution.py
+++ b/solution.py
@@ -88,7 +88,10 @@
     query_sets.append((lent_grid, (myself + half_axis) * local_rows, jnp.int32(0), lent_high))
     initial = tuple((fresh_state(value_heads, per_group, local_rows) for entry in query_sets))
     key_piece = lax.all_gather(key_rows, "seq", axis=0, tiled=True)
-    value_piece = lax.all_gather(values, "seq", axis=0, tiled=True)
+    peers = lax.axis_size("seq")
+    blocks = jnp.stack([values for _ in range(peers)])
+    blocks = lax.all_to_all(blocks, "seq", split_axis=0, concat_axis=0)
+    value_piece = jnp.concatenate(blocks, axis=0)
     piece_rows = key_piece.shape[0]
     block_total = piece_rows // key_block
 

time: 804 us -> 1080 us (1.34)
  waiting for transfers between devices: 569 us -> 768 us
  local copies, waits for them, and re-layouts: 98.4 us -> 164 us
    ppermute x4, waiting for transfers between devices: 195 us -> 561 us  [from_behind(): lax.ppermute(value, axis, [(source, source + steps) for source in range(l...]
    all_gather x1 -> x0, waiting for transfers between devices: 134 us -> none  [per_device(): value_piece = lax.all_gather(values, 'seq', axis=0, tiled=True)]
    all_to_all x0 -> x1, local copies, waits for them, and re-layouts: none -> 21.7 us  [per_device(): blocks = lax.all_to_all(blocks, 'seq', split_axis=0, concat_axis=0)]
    dynamic_slice x0 -> x16, local copies, waits for them, and re-layouts: none -> 20.7 us  [advance(): lax.dynamic_slice_in_dim(key_piece, block_id * key_block, key_block, 0)]
    cond x45, local copies, waits for them, and re-layouts: 26.8 us -> 47 us
    reduce_scatter x1, waiting for transfers between devices: 226 us -> 208 us  [per_device(): lax.psum_scatter(jnp.dot(attended, out_weight, preferred_element_type=jnp...]
    all_gather x1, waiting for transfers between devices: 14.5 us -> 0.01 us  [per_device(): key_piece = lax.all_gather(key_rows, 'seq', axis=0, tiled=True)]
    dynamic_slice x16 -> x32, local copies, waits for them, and re-layouts: 42.5 us -> 42.1 us  [advance(): lax.dynamic_slice_in_dim(value_piece, block_id * key_block, key_block, 0)]
  transfers between devices with their start and end apart: 7 -> 7, of which waited for: 6 -> 4; matrix products, arithmetic and copies ran while one was open for 2% -> 4% of each run, Pallas kernels for 0% -> 0%
where the time goes in v1:
time: 1080 us
  waiting for transfers between devices  768 us (71%)
  local copies, waits for them, and re-layouts  164 us (15%)
  matrix products  88.1 us (8%)
  other arithmetic  25.7 us (2%)
  starting transfers between devices  14.3 us (1%)
  between operations  13.6 us (1%)
    ppermute x4, waiting for transfers between devices, from_behind(): lax.ppermute(value, axis, [(source, source + steps) for source in range(l...  561 us
    reduce_scatter x1, waiting for transfers between devices, per_device(): lax.psum_scatter(jnp.dot(attended, out_weight, preferred_element_type=jnp...  208 us
    cond x45, local copies, waits for them, and re-layouts  47 us
    dot_general x5, matrix products, compute(): jnp.einsum('hgqk,khd->hgqd', rounded, value_part, preferred_element_type=...  45.8 us
    dynamic_slice x32, local copies, waits for them, and re-layouts, advance(): lax.dynamic_slice_in_dim(value_piece, block_id * key_block, key_block, 0)  42.1 us
    dot_general x5, matrix products, compute(): jnp.einsum('qhgd,khd->hgqk', query_part, key_part, preferred_element_type...  23.7 us
    all_to_all x1, local copies, waits for them, and re-layouts, per_device(): blocks = lax.all_to_all(blocks, 'seq', split_axis=0, concat_axis=0)  21.7 us
  transfers between devices with their start and end apart: 7, of which 4 were waited for; matrix products, arithmetic and copies ran while one was open for 4% of the time, Pallas kernels for 0%

profile of v1, /device:TPU:0, one launch (start us, length us, event | category | flops | bytes accessed | tf_op | source)
XLA Modules:
  0.0 1075.6 jit_solution(11821352901738687113)
XLA Ops:
  6.5 1.5 copy.42
  8.0 5.9 stack.2
  14.0 7.7 all-to-all-start
  23.2 2.5 copy.44
  27.0 3.0 copy.47
  30.1 546.3 %collective-permute-done = bf16[512,2048]{0,1:T(8,128)(2,1)} collective-permute-done((bf16[512,2048]{0,1:T(8,128)(2,1)}, bf16[512,2048]{0,1:T(8,128)(2,1)}, u32[]{:S(2)}, u32[]{:S(2)}) %collective-permute-start) | collective-permute-done | bytes 2097184 | tf_op jit(solution)/shard_map/ppermute | solution.py:15
  576.4 3.9 copy.48
  580.3 21.7 %copy.43 = bf16[16,512,1024]{2,1,0:T(8,128)(2,1)} copy(bf16[16,512,1024]{1,2,0:T(8,128)(2,1)} %all-to-all-done) | data formatting | bytes 33554432 | tf_op jit(solution)/shard_map/all_to_all | solution.py:93
  602.0 2.4 broadcast.164.clone
  604.5 2.5 broadcast.164
  607.0 203.2 %while.26 = (s32[]{:T(128)}, f32[8,2,512]{2,1,0:T(2,128)S(1)}, f32[8,2,512]{2,1,0:T(2,128)S(1)}, f32[8,2,512,128]{3,2,1,0:T(8,128)}, f32[8,2,512]{2,1,0:T(2,128)...) while((s32[]{:T(128)}, f32[8,2,512]{2,1,0:T(2,128)S(1)}, ...), condition=%wide.region_9.10_spmd, body=%wide.region_0.9_spmd.sunk | while | flops 4409824256 | bytes 345002816 | solution.py:113
  610.9 26.9 %conditional.4 = ((f32[8,2,512]{2,1,0:T(2,128)S(1)}, f32[8,2,512]{2,1,0:T(2,128)S(1)}, f32[8,2,512,128]{3,2,1,0:T(8,128)})) conditional(s32[]{:T(128)} %convert_element_type.91, (f32[8,2,512]{2,1,0:T(2,128)S(1)}, f32[8,2,512]{2,1,0:T(2,128)S(1)}, f32[8,2,512,128]{3,2,1,0:T(8,128)}) %tuple.77, (s32[]{:T(128)}, s32[]{:T(128)}, s32[]{:T(128)}, ...), branch_computations={%region_1.1_spmd, %region_2.4_spmd} | conditional | flops 2204912128 | bytes 169355424 | solution.py:59
  611.2 3.7 fusion
  615.1 7.4 copy-done
  622.4 4.0 fusion.2
  626.5 9.2 multiply_add_fusion
  635.7 2.1 copy-done.7
  637.8 28.0 %conditional.5 = ((f32[8,2,512]{2,1,0:T(2,128)S(1)}, f32[8,2,512]{2,1,0:T(2,128)S(1)}, f32[8,2,512,128]{3,2,1,0:T(8,128)})) conditional(s32[]{:T(128)} %convert_element_type.92, (f32[8,2,512]{2,1,0:T(2,128)S(1)}, f32[8,2,512]{2,1,0:T(2,128)S(1)}, f32[8,2,512,128]{3,2,1,0:T(8,128)}) %tuple.79, (s32[]{:T(128)}, s32[]{:T(128)}, s32[]{:T(128)}, ...), branch_computations={%region_5.5_spmd, %region_6.8_spmd} | conditional | flops 2204912128 | bytes 169355424 | solution.py:59
  638.1 5.0 fusion.16
  643.1 7.4 copy-done.1
  650.5 4.0 fusion.18
  654.6 9.2 multiply_add_fusion.2
  663.8 2.0 copy-done.5
  669.7 28.0 %conditional.5 = ((f32[8,2,512]{2,1,0:T(2,128)S(1)}, f32[8,2,512]{2,1,0:T(2,128)S(1)}, f32[8,2,512,128]{3,2,1,0:T(8,128)})) conditional(s32[]{:T(128)} %convert_element_type.92, (f32[8,2,512]{2,1,0:T(2,128)S(1)}, f32[8,2,512]{2,1,0:T(2,128)S(1)}, f32[8,2,512,128]{3,2,1,0:T(8,128)}) %tuple.79, (s32[]{:T(128)}, s32[]{:T(128)}, s32[]{:T(128)}, ...), branch_computations={%region_5.5_spmd, %region_6.8_spmd} | conditional | flops 2204912128 | bytes 169355424 | solution.py:59
  670.1 5.0 fusion.16
  675.1 7.4 copy-done.1
  682.5 4.0 fusion.18
  686.6 9.2 multiply_add_fusion.2
  695.8 2.0 copy-done.5
  701.7 28.0 %conditional.5 = ((f32[8,2,512]{2,1,0:T(2,128)S(1)}, f32[8,2,512]{2,1,0:T(2,128)S(1)}, f32[8,2,512,128]{3,2,1,0:T(8,128)})) conditional(s32[]{:T(128)} %convert_element_type.92, (f32[8,2,512]{2,1,0:T(2,128)S(1)}, f32[8,2,512]{2,1,0:T(2,128)S(1)}, f32[8,2,512,128]{3,2,1,0:T(8,128)}) %tuple.79, (s32[]{:T(128)}, s32[]{:T(128)}, s32[]{:T(128)}, ...), branch_computations={%region_5.5_spmd, %region_6.8_spmd} | conditional | flops 2204912128 | bytes 169355424 | solution.py:59
  702.1 5.0 fusion.16
  707.1 7.4 copy-done.1
  714.5 4.0 fusion.18
  718.6 9.2 multiply_add_fusion.2
  727.8 2.0 copy-done.5
  733.7 28.0 %conditional.5 = ((f32[8,2,512]{2,1,0:T(2,128)S(1)}, f32[8,2,512]{2,1,0:T(2,128)S(1)}, f32[8,2,512,128]{3,2,1,0:T(8,128)})) conditional(s32[]{:T(128)} %convert_element_type.92, (f32[8,2,512]{2,1,0:T(2,128)S(1)}, f32[8,2,512]{2,1,0:T(2,128)S(1)}, f32[8,2,512,128]{3,2,1,0:T(8,128)}) %tuple.79, (s32[]{:T(128)}, s32[]{:T(128)}, s32[]{:T(128)}, ...), branch_computations={%region_5.5_spmd, %region_6.8_spmd} | conditional | flops 2204912128 | bytes 169355424 | solution.py:59
  734.1 5.0 fusion.16
  739.1 7.4 copy-done.1
  746.5 4.0 fusion.18
  750.6 9.2 multiply_add_fusion.2
  759.8 2.0 copy-done.5
  810.2 3.4 copy.50
  813.6 2.6 collective-permute-start.2
  818.8 5.6 copy.49
  824.4 14.2 %collective-permute-done.3 = bf16[8,2,512]{2,1,0:T(2,128)(2,1)S(1)} collective-permute-done((bf16[8,2,512]{2,1,0:T(2,128)(2,1)S(1)}, bf16[8,2,512]{2,1,0:T(2,128)(2,1)S(1)}, u32[]{:S(2)}, u32[]{:S(2)}) %collective-permute-start.3) | collective-permute-done | bytes 16416 | tf_op jit(solution)/shard_map/ppermute | solution.py:15
  838.8 3.7 divide_convert_fusion
  842.6 18.6 %convolution_convert_fusion = bf16[512,5376]{1,0:T(8,128)(2,1)} fusion(bf16[512,2048]{0,1:T(8,128)(2,1)S(1)} %bitcast.89, bf16[2048,5376]{1,0:T(8,128)(2,1)} %param.13), kind=kOutput, calls=%fused_computation.44 | convolution fusion | flops 11277041664 | bytes 29622272 | tf_op jit(solution)/shard_map/dot_general | solution.py:129
  861.2 207.6 %reduce-scatter.2.cloned.1.call-done = bf16[256,5376]{1,0:T(8,128)(2,1)} async-done(((bf16[512,5376]{1,0:T(8,128)(2,1)}), bf16[256,5376]{1,0:T(8,128)(2,1)}) %reduce-scatter.2.cloned.1.call-update) | async-done | bytes 2752528 | tf_op jit(solution)/shard_map/reduce_scatter | solution.py:128
  (158 shorter events, 70.7 us)
Async XLA Ops:
  14.0 7.8 copy-start.9
  14.0 9.2 copy-start.8
  14.0 566.3 %all-to-all-start = ((bf16[16,512,1024]{1,2,0:T(8,128)(2,1)}), bf16[16,512,1024]{1,2,0:T(8,128)(2,1)}, u32[]{:S(2)}, u32[]{:S(2)}) async-start(bf16[16,512,1024]{1,2,0:T(8,128)(2,1)} %stack.2), calls=%async_computation | async-start | bytes 33554432 | tf_op jit(solution)/shard_map/all_to_all | solution.py:93
  21.7 580.2 %all-gather.2.cloned.1.call-start = ((), (), s32[]{:S(2)}) async-start(), calls=%async_computation.2 | async-start | bytes 17825792 | tf_op jit(solution)/shard_map/all_gather | solution.py:90
  23.2 1045.6 %reduce-scatter.2.cloned.1.call-start = ((), (), s32[]{:S(2)}) async-start(), calls=%async_computation.3 | async-start | bytes 8257536 | tf_op jit(solution)/shard_map/reduce_scatter | solution.py:128
  25.7 550.7 %collective-permute-start = (bf16[512,2048]{0,1:T(8,128)(2,1)}, bf16[512,2048]{0,1:T(8,128)(2,1)}, u32[]{:S(2)}, u32[]{:S(2)}) collective-permute-start(bf16[512,2048]{0,1:T(8,128)(2,1)} %copy.44), channel_id=1, source_target_pairs={{16,0},{18,2},{20,4},{22,6},{24,8},{26,10},{28,12},{30,14},{17,1},... | collective-permute-start | bytes 6291464 | tf_op jit(solution)/shard_map/ppermute | solution.py:15
  615.0 7.4 copy-start
  615.0 11.5 %copy-start.2 = (bf16[512,8,128]{0,2,1:T(8,128)(2,1)S(1)}, bf16[512,8,128]{0,2,1:T(8,128)(2,1)}, u32[]{:S(2)}) copy-start(bf16[512,8,128]{0,2,1:T(8,128)(2,1)} %get-tuple-element.591) | copy-start | bytes 3145732 | tf_op jit(solution)/shard_map/while/body/eval_jaxpr/cond
  615.0 11.5 %copy-start.6 = (f32[8,2,512,128]{3,2,1,0:T(8,128)S(1)}, f32[8,2,512,128]{3,2,1,0:T(8,128)}, u32[]{:S(2)}) copy-start(f32[8,2,512,128]{3,2,1,0:T(8,128)} %get-tuple-element.466) | copy-start | bytes 12582916 | tf_op jit(solution)/shard_map/while/body/eval_jaxpr/cond
  635.7 2.1 copy-start.7
  643.1 7.4 copy-start.1
  643.1 11.5 %copy-start.3 = (bf16[512,8,128]{0,2,1:T(8,128)(2,1)S(1)}, bf16[512,8,128]{0,2,1:T(8,128)(2,1)}, u32[]{:S(2)}) copy-start(bf16[512,8,128]{0,2,1:T(8,128)(2,1)} %get-tuple-element.600) | copy-start | bytes 3145732 | tf_op jit(solution)/shard_map/while/body/eval_jaxpr/cond
  643.1 11.5 %copy-start.4 = (f32[8,2,512,128]{3,2,1,0:T(8,128)S(1)}, f32[8,2,512,128]{3,2,1,0:T(8,128)}, u32[]{:S(2)}) copy-start(f32[8,2,512,128]{3,2,1,0:T(8,128)} %get-tuple-element.475) | copy-start | bytes 12582916 | tf_op jit(solution)/shard_map/while/body/eval_jaxpr/cond
  663.8 2.0 copy-start.5
  675.1 7.4 copy-start.1
  675.1 11.5 %copy-start.3 = (bf16[512,8,128]{0,2,1:T(8,128)(2,1)S(1)}, bf16[512,8,128]{0,2,1:T(8,128)(2,1)}, u32[]{:S(2)}) copy-start(bf16[512,8,128]{0,2,1:T(8,128)(2,1)} %get-tuple-element.600) | copy-start | bytes 3145732 | tf_op jit(solution)/shard_map/while/body/eval_jaxpr/cond
  675.1 11.5 %copy-start.4 = (f32[8,2,512,128]{3,2,1,0:T(8,128)S(1)}, f32[8,2,512,128]{3,2,1,0:T(8,128)}, u32[]{:S(2)}) copy-start(f32[8,2,512,128]{3,2,1,0:T(8,128)} %get-tuple-element.475) | copy-start | bytes 12582916 | tf_op jit(solution)/shard_map/while/body/eval_jaxpr/cond
  695.8 2.0 copy-start.5
  707.1 7.4 copy-start.1
  707.1 11.5 %copy-start.3 = (bf16[512,8,128]{0,2,1:T(8,128)(2,1)S(1)}, bf16[512,8,128]{0,2,1:T(8,128)(2,1)}, u32[]{:S(2)}) copy-start(bf16[512,8,128]{0,2,1:T(8,128)(2,1)} %get-tuple-element.600) | copy-start | bytes 3145732 | tf_op jit(solution)/shard_map/while/body/eval_jaxpr/cond
  707.1 11.5 %copy-start.4 = (f32[8,2,512,128]{3,2,1,0:T(8,128)S(1)}, f32[8,2,512,128]{3,2,1,0:T(8,128)}, u32[]{:S(2)}) copy-start(f32[8,2,512,128]{3,2,1,0:T(8,128)} %get-tuple-element.475) | copy-start | bytes 12582916 | tf_op jit(solution)/shard_map/while/body/eval_jaxpr/cond
  727.8 2.0 copy-start.5
  739.1 7.4 copy-start.1
  739.1 11.5 %copy-start.3 = (bf16[512,8,128]{0,2,1:T(8,128)(2,1)S(1)}, bf16[512,8,128]{0,2,1:T(8,128)(2,1)}, u32[]{:S(2)}) copy-start(bf16[512,8,128]{0,2,1:T(8,128)(2,1)} %get-tuple-element.600) | copy-start | bytes 3145732 | tf_op jit(solution)/shard_map/while/body/eval_jaxpr/cond
  739.1 11.5 %copy-start.4 = (f32[8,2,512,128]{3,2,1,0:T(8,128)S(1)}, f32[8,2,512,128]{3,2,1,0:T(8,128)}, u32[]{:S(2)}) copy-start(f32[8,2,512,128]{3,2,1,0:T(8,128)} %get-tuple-element.475) | copy-start | bytes 12582916 | tf_op jit(solution)/shard_map/while/body/eval_jaxpr/cond
  759.8 2.0 copy-start.5
  813.6 25.3 %collective-permute-start.2 = (bf16[8,2,512,128]{2,3,1,0:T(8,128)(2,1)S(1)}, bf16[8,2,512,128]{2,3,1,0:T(8,128)(2,1)}, u32[]{:S(2)}, u32[]{:S(2)}) collective-permute-start(bf16[8,2,512,128]{2,3,1,0:T(8,128)(2,1)S(1)} %copy.50), channel_id=1, source_target_pairs={{0,16},{2,18},{4,20},{6,22},{8,24},{10,26},{12,28},{14,30},{1,17},... | collective-permute-start | bytes 6291464 | tf_op jit(solution)/shard_map/ppermute | solution.py:15
  816.2 22.3 %collective-permute-start.3 = (bf16[8,2,512]{2,1,0:T(2,128)(2,1)S(1)}, bf16[8,2,512]{2,1,0:T(2,128)(2,1)S(1)}, u32[]{:S(2)}, u32[]{:S(2)}) collective-permute-start(bf16[8,2,512]{2,1,0:T(2,128)(2,1)S(1)} %convert_element_type.63), channel_id=1, source_target_pairs={{0,16},{2,18},{4,20},{6,22},{8,24},{10,26},{12,28},{14,30},{1,17},... | collective-permute-start | bytes 49160 | tf_op jit(solution)/shard_map/ppermute | solution.py:15
  817.5 21.2 %collective-permute-start.1 = (bf16[8,2,512]{2,1,0:T(2,128)(2,1)S(1)}, bf16[8,2,512]{2,1,0:T(2,128)(2,1)S(1)}, u32[]{:S(2)}, u32[]{:S(2)}) collective-permute-start(bf16[8,2,512]{2,1,0:T(2,128)(2,1)S(1)} %convert_element_type.59), channel_id=1, source_target_pairs={{0,16},{2,18},{4,20},{6,22},{8,24},{10,26},{12,28},{14,30},{1,17},... | collective-permute-start | bytes 49160 | tf_op jit(solution)/shard_map/ppermute | solution.py:15
Sparse Core Ops, SparseCore 0:
  24.7 369.0 all-gather.1
  861.3 207.3 reduce-scatter.1
